TPU v7x, 32 devices: a whole 2x2x4 slice. The times are simulated.
32 devices in a mesh: dp: 4 (over z), seq: 8 (over y, x, core).
Axes of the slice: x: 2, y: 2, z: 4, core: 2. Of those that a mesh axis runs over, the one named last changes fastest.
Arguments:
- saved_codes: bfloat16 [4, 1024, 1536], P('dp', 'seq'), may hold values from -6 to 6
- code_scales: float32 [4, 12, 1024], P('dp', None, 'seq'), may hold values from 0.25 to 4
- lengths: int32 [4], replicated, may hold values from 128 to 1024, as said below
- in_weight: bfloat16 [3072, 1536], P('dp'), may hold values from -0.15625 to 0.15625
- conv_kernel: float32 [31, 1536], replicated, may hold values from -1 to 1
- bn_gain: float32 [1536], replicated, may hold values from 0.1 to 1.9
- bn_shift: float32 [1536], replicated, may hold values from -3 to 3
- out_grad: bfloat16 [4, 1024, 1536], P('dp', 'seq'), may hold values from -6 to 6
Outputs:
- in_grad: bfloat16 [4, 1024, 1536], P('dp', 'seq')
- weight_grad: float32 [3072, 1536], P('dp')
- kernel_grad: float32 [31, 1536], replicated
- gain_grad: float32 [1536], replicated
- shift_grad: float32 [1536], replicated
Inputs may be any that keep to these rules, and one draw needn't show every extreme that they name: `lengths`: at least one recording has exactly 1024 valid frames.
All inputs are finite; a program needn't handle non-finite values.
Results may differ from a plain program's by a relative error of at most 0.0067.
Values may be sent and summed in bfloat16 or wider, within the bound.
A program may use at most 128 MiB of HBM per device.

v0:
```python
import jax
import jax.numpy as jnp
from jax import lax
from jax.sharding import PartitionSpec as P

EPS = 1e-05


def padded_2(cells, sides, width):
    for axis, dim in sides:
        count = lax.axis_size(axis)
        ends = count - 1
        head = lax.slice_in_dim(cells, 0, width, axis=dim)
        tail = lax.slice_in_dim(cells, cells.shape[dim] - width, cells.shape[dim], axis=dim)
        cells = jnp.concatenate(
            [
                lax.ppermute(tail, axis, [(i, (i + 1) % count) for i in range(ends)]),
                cells,
                lax.ppermute(head, axis, [((i + 1) % count, i) for i in range(ends)]),
            ],
            axis=dim,
        )
    return cells


def restore(quantized, scales):
    per_channel = jnp.repeat(scales.T, 128, axis=1)
    return (quantized.astype(jnp.float32) * per_channel).astype(jnp.bfloat16)


def depthwise(padded, kernel, frames):
    running = jnp.zeros((frames, padded.shape[1]), jnp.float32)
    for offset in range(kernel.shape[0]):
        running = running + kernel[offset] * padded[offset : offset + frames].astype(jnp.float32)
    return running


def per_device(
    saved_codes, code_scales, lengths, in_weight, conv_kernel, bn_gain, bn_shift, out_grad
):
    frames = saved_codes.shape[1]
    feature_width = saved_codes.shape[2]
    tap_count = conv_kernel.shape[0]
    half_span = (tap_count - 1) // 2
    groups = lengths.shape[0]
    group_at = lax.axis_index("dp")
    length = jnp.sum(jnp.where(jnp.arange(groups, dtype=jnp.int32) == group_at, lengths, 0))
    counted = jnp.sum(lengths).astype(jnp.float32)
    first_frame = lax.axis_index("seq") * frames
    valid_mask = (first_frame + jnp.arange(frames, dtype=jnp.int32) < length).astype(jnp.float32)[
        :, None
    ]
    restored = restore(saved_codes[0], code_scales[0])
    weights = lax.all_gather(in_weight, "dp", axis=0, tiled=True)
    pre_act = lax.dot_general(
        restored, weights, (((1,), (1,)), ((), ())), preferred_element_type=jnp.float32
    )
    linear = pre_act[:, :feature_width]
    gate_part = jax.nn.sigmoid(pre_act[:, feature_width:])
    gated = (linear * gate_part * valid_mask).astype(jnp.bfloat16)
    gated_pad = padded_2(gated, (("seq", 0),), half_span)
    conv_out = depthwise(gated_pad, conv_kernel, frames)
    mean_value = lax.psum(jnp.sum(conv_out * valid_mask, axis=0), ("dp", "seq")) / counted
    centered = (conv_out - mean_value) * valid_mask
    variance = lax.psum(jnp.sum(centered * centered, axis=0), ("dp", "seq")) / counted
    inverse = lax.rsqrt(variance + EPS)
    normed = (conv_out - mean_value) * inverse
    shaped = bn_gain * normed + bn_shift
    smooth = jax.nn.sigmoid(shaped)
    grad_shaped = (
        out_grad[0].astype(jnp.float32) * valid_mask * smooth * (1.0 + shaped * (1.0 - smooth))
    )
    shift_grad, gain_grad = lax.psum(
        (jnp.sum(grad_shaped, axis=0), jnp.sum(grad_shaped * normed, axis=0)), ("dp", "seq")
    )
    grad_conv = (
        bn_gain * inverse * (grad_shaped - (shift_grad + normed * gain_grad) / counted) * valid_mask
    )
    kernel_part = jnp.stack(
        [
            jnp.sum(grad_conv * gated_pad[offset : offset + frames].astype(jnp.float32), axis=0)
            for offset in range(tap_count)
        ]
    )
    kernel_grad = lax.psum(kernel_part, ("dp", "seq"))
    grad_pad = padded_2(grad_conv, (("seq", 0),), half_span)
    grad_gated = depthwise(grad_pad, conv_kernel[::-1], frames) * valid_mask
    grad_pre = jnp.concatenate(
        [grad_gated * gate_part, grad_gated * linear * gate_part * (1.0 - gate_part)], axis=1
    ).astype(jnp.bfloat16)
    in_grad = jnp.dot(grad_pre, weights, preferred_element_type=jnp.float32)
    own_columns = lax.all_to_all(grad_pre[None], "dp", split_axis=2, concat_axis=0, tiled=True)
    local_rows = lax.dot_general(
        own_columns,
        lax.all_gather(restored[None], "dp", axis=0, tiled=True),
        (((0, 1), (0, 1)), ((), ())),
        preferred_element_type=jnp.float32,
    )
    weight_grad = lax.psum(local_rows, "seq")
    return (in_grad.astype(jnp.bfloat16)[None], weight_grad, kernel_grad, gain_grad, shift_grad)


def solution(mesh):
    in_specs = (
        P("dp", "seq", None),
        P("dp", None, "seq"),
        P(),
        P("dp", None),
        P(),
        P(),
        P(),
        P("dp", "seq", None),
    )
    out_specs = (P("dp", "seq", None), P("dp", None), P(), P(), P())
    return jax.shard_map(
        per_device, mesh=mesh, in_specs=in_specs, out_specs=out_specs, check_vma=False
    )
```

profile of v0, /device:TPU:0, one launch (start us, length us, event | category | flops | bytes accessed | tf_op | source)
XLA Modules:
  0.0 607.7 jit_solution(5439914261031607796)
XLA Ops:
  10.8 168.2 %all-gather.3.cloned.1.call-done = bf16[3072,1536]{1,0:T(8,128)(2,1)} async-done(((bf16[768,1536]{1,0:T(8,128)(2,1)}), bf16[3072,1536]{1,0:T(8,128)(2,1)}) %all-gather.3.cloned.1.call-update) | async-done | bytes 9437200 | tf_op jit(solution)/shard_map/all_gather | solution.py:54
  179.1 6.9 %fusion.199 = f32[128,3072]{1,0:T(8,128)S(1)} fusion(bf16[128,1536]{0,1:T(8,128)(2,1)S(1)} %fusion.150, bf16[3072,1536]{1,0:T(8,128)(2,1)} %all-gather.3.cloned.1.call-done), kind=kOutput, calls=%fused_computation.398 | convolution fusion | flops 1207959552 | bytes 11403264 | tf_op jit(solution)/shard_map/dot_general | solution.py:55
  186.2 1.4 collective-permute-start.1
  187.7 3.0 collective-permute-start
  192.3 5.1 multiply_reduce_fusion.2
  197.4 40.2 %psum.42 = f32[1536]{0:T(1024)S(1)} all-reduce(f32[1536]{0:T(1024)S(1)} %get-tuple-element.78), channel_id=1, replica_groups=mesh['dp'=4,'seq'=8] {'dp','seq'}, use_global_device_ids=true, to_apply=%region_2.3 | all-reduce | flops 1536 | bytes 12288 | tf_op jit(solution)/shard_map/psum | solution.py:63
  237.8 42.5 %psum.43 = f32[1536]{0:T(1024)S(1)} all-reduce(f32[1536]{0:T(1024)S(1)} %multiply_reduce_fusion.1), channel_id=1, replica_groups=mesh['dp'=4,'seq'=8] {'dp','seq'}, use_global_device_ids=true, to_apply=%region_5.6 | all-reduce | flops 1536 | bytes 12288 | tf_op jit(solution)/shard_map/psum | solution.py:65
  280.3 1.3 fusion.195
  281.6 1.2 fusion.192
  282.9 38.3 %all-reduce = (f32[1536]{0:T(1024)}, f32[1536]{0:T(1024)}) all-reduce(f32[1536]{0:T(1024)S(1)} %get-tuple-element.36, f32[1536]{0:T(1024)S(1)} %get-tuple-element.35), channel_id=1, replica_groups=mesh['dp'=4,'seq'=8] {'dp','seq'}, use_global_device_ids=true, to_apply=%region_9.10 | all-reduce | flops 3072 | bytes 24576 | tf_op jit(solution)/shard_map/psum | solution.py:73
  321.1 3.8 fusion.148
  324.9 1.3 collective-permute-start.3
  326.2 3.2 collective-permute-start.2
  331.5 5.4 multiply_convert_fusion.1
  338.0 1.9 copy.22
  340.5 17.0 %reduce.62 = bf16[3072,128]{1,0:T(8,128)(2,1)S(1)} reduce(bf16[3072,1,128]{2,1,0:T(2,128)(2,1)S(1)} %bitcast.43, bf16[]{:T(256)} %broadcast.68), dimensions={1}, to_apply=%bitcast.34.reduce_sub_computation | reduce | bytes 1572866
  358.4 3.5 all-to-all-start
  365.3 2.8 stack.127
  368.3 18.3 %all-to-all-done = bf16[4,2,49152]{2,1,0:T(2,128)(2,1)S(1)} async-done(((bf16[4,2,49152]{2,1,0:T(2,128)(2,1)}), bf16[4,2,49152]{2,1,0:T(2,128)(2,1)S(1)}, u32[]{:S(2)}, u32[]{:S(2)}) %all-to-all-start) | async-done | bytes 786464 | tf_op jit(solution)/shard_map/all_to_all | solution.py:92
  387.5 4.4 convolution_bitcast_fusion
  393.0 5.8 fusion
  398.9 105.5 %all-reduce.6.cloned.1.call-done = f32[31,1536]{1,0:T(8,128)} async-done(((f32[31,1536]{1,0:T(8,128)}), f32[31,1536]{1,0:T(8,128)}) %all-reduce.6.cloned.1.call-update) | async-done | bytes 190480 | tf_op jit(solution)/shard_map/psum | solution.py:85
  504.4 91.3 %all-reduce.4.cloned.1.call-done = f32[768,1536]{1,0:T(8,128)} async-done(((f32[768,1536]{1,0:T(8,128)}), f32[768,1536]{1,0:T(8,128)}) %all-reduce.4.cloned.1.call-update) | async-done | bytes 4718608 | tf_op jit(solution)/shard_map/psum | solution.py:99
  595.7 4.8 copy.30
  (150 shorter events, 15.3 us)
Async XLA Ops:
  7.2 171.9 %all-gather.3.cloned.1.call-start = ((), (), s32[]{:S(2)}) async-start(), calls=%async_computation.1 | async-start | bytes 11796480 | tf_op jit(solution)/shard_map/all_gather | solution.py:54
  7.9 379.6 %all-gather.5.cloned.1.call-start = ((), (), s32[]{:S(2)}) async-start(), calls=%async_computation.2 | async-start | bytes 1966080 | tf_op jit(solution)/shard_map/all_gather | solution.py:95
  8.4 170.7 %copy-start = (bf16[1,128,1536]{1,2,0:T(8,128)(2,1)}, bf16[1,128,1536]{1,2,0:T(8,128)(2,1)S(1)}, u32[]{:S(2)}) copy-start(bf16[1,128,1536]{1,2,0:T(8,128)(2,1)S(1)} %copy.21) | copy-start | bytes 1179652
  9.8 176.1 %copy-start.37 = (f32[128]{0:T(128)}, f32[128]{0:T(128)S(1)}, u32[]{:S(2)}) copy-start(f32[128]{0:T(128)S(1)} %compare_convert_fusion) | copy-start | bytes 1540
  10.8 181.5 %copy-start.13 = (f32[1536]{0:T(1024)}, f32[1536]{0:T(1024)S(1)}, u32[]{:S(2)}) copy-start(f32[1536]{0:T(1024)S(1)} %get-tuple-element.38) | copy-start | bytes 18436
  10.8 181.5 %copy-start.15 = (f32[1536]{0:T(1024)}, f32[1536]{0:T(1024)S(1)}, u32[]{:S(2)}) copy-start(f32[1536]{0:T(1024)S(1)} %get-tuple-element.39) | copy-start | bytes 18436
  10.8 181.5 %copy-start.16 = (f32[1536]{0:T(1024)}, f32[1536]{0:T(1024)S(1)}, u32[]{:S(2)}) copy-start(f32[1536]{0:T(1024)S(1)} %get-tuple-element.40) | copy-start | bytes 18436
  10.8 181.5 %copy-start.17 = (f32[1536]{0:T(1024)}, f32[1536]{0:T(1024)S(1)}, u32[]{:S(2)}) copy-start(f32[1536]{0:T(1024)S(1)} %get-tuple-element.41) | copy-start | bytes 18436
  10.8 181.5 %copy-start.18 = (f32[1536]{0:T(1024)}, f32[1536]{0:T(1024)S(1)}, u32[]{:S(2)}) copy-start(f32[1536]{0:T(1024)S(1)} %get-tuple-element.42) | copy-start | bytes 18436
  10.8 181.5 %copy-start.19 = (f32[1536]{0:T(1024)}, f32[1536]{0:T(1024)S(1)}, u32[]{:S(2)}) copy-start(f32[1536]{0:T(1024)S(1)} %get-tuple-element.43) | copy-start | bytes 18436
  10.8 181.5 %copy-start.20 = (f32[1536]{0:T(1024)}, f32[1536]{0:T(1024)S(1)}, u32[]{:S(2)}) copy-start(f32[1536]{0:T(1024)S(1)} %get-tuple-element.44) | copy-start | bytes 18436
  10.8 181.5 %copy-start.21 = (f32[1536]{0:T(1024)}, f32[1536]{0:T(1024)S(1)}, u32[]{:S(2)}) copy-start(f32[1536]{0:T(1024)S(1)} %get-tuple-element.45) | copy-start | bytes 18436
  10.8 181.5 %copy-start.22 = (f32[1536]{0:T(1024)}, f32[1536]{0:T(1024)S(1)}, u32[]{:S(2)}) copy-start(f32[1536]{0:T(1024)S(1)} %get-tuple-element.46) | copy-start | bytes 18436
  10.8 181.5 %copy-start.23 = (f32[1536]{0:T(1024)}, f32[1536]{0:T(1024)S(1)}, u32[]{:S(2)}) copy-start(f32[1536]{0:T(1024)S(1)} %get-tuple-element.47) | copy-start | bytes 18436
  10.8 181.5 %copy-start.24 = (f32[1536]{0:T(1024)}, f32[1536]{0:T(1024)S(1)}, u32[]{:S(2)}) copy-start(f32[1536]{0:T(1024)S(1)} %get-tuple-element.48) | copy-start | bytes 18436
  10.8 181.5 %copy-start.25 = (f32[1536]{0:T(1024)}, f32[1536]{0:T(1024)S(1)}, u32[]{:S(2)}) copy-start(f32[1536]{0:T(1024)S(1)} %get-tuple-element.49) | copy-start | bytes 18436
  10.8 181.5 %copy-start.26 = (f32[1536]{0:T(1024)}, f32[1536]{0:T(1024)S(1)}, u32[]{:S(2)}) copy-start(f32[1536]{0:T(1024)S(1)} %get-tuple-element.50) | copy-start | bytes 18436
  186.2 5.9 collective-permute-start.1
  187.7 4.5 collective-permute-start
  324.9 6.6 %collective-permute-start.3 = (f32[15,1536]{1,0:T(8,128)S(1)}, f32[15,1536]{1,0:T(8,128)S(1)}, u32[]{:S(2)}, u32[]{:S(2)}) collective-permute-start(f32[15,1536]{1,0:T(8,128)S(1)} %get-tuple-element.81), channel_id=1, source_target_pairs={{1,0},{2,1},{3,2},{4,3},{5,4},{6,5},{7,6},{9,8},{10,9},{11,10},{12... | collective-permute-start | bytes 276488 | tf_op jit(solution)/shard_map/ppermute | solution.py:19
  326.2 5.3 collective-permute-start.2
  358.4 28.2 %all-to-all-start = ((bf16[4,2,49152]{2,1,0:T(2,128)(2,1)}), bf16[4,2,49152]{2,1,0:T(2,128)(2,1)S(1)}, u32[]{:S(2)}, u32[]{:S(2)}) async-start(bf16[4,2,49152]{2,1,0:T(2,128)(2,1)} %reshape.100), calls=%async_computation | async-start | bytes 1572864 | tf_op jit(solution)/shard_map/all_to_all | solution.py:92
  361.9 142.4 %all-reduce.6.cloned.1.call-start = ((), (), s32[]{:S(2)}) async-start(), calls=%async_computation.4 | async-start | bytes 393216 | tf_op jit(solution)/shard_map/psum | solution.py:85
  368.1 227.6 %all-reduce.4.cloned.1.call-start = ((), (), s32[]{:S(2)}) async-start(), calls=%async_computation.3 | async-start | bytes 9437184 | tf_op jit(solution)/shard_map/psum | solution.py:99
  (26 other events, 503.1 us)
Sparse Core Ops, SparseCore 0:
  9.6 169.4 all-gather.2
  331.6 44.2 all-gather.4
  382.1 122.2 all-reduce.5
  508.1 87.5 all-reduce.3
where the time goes:
time: 609 us; the launch traced here: 608 us
  waiting for transfers between devices  384 us (63%)
  blocking collectives  121 us (20%)
  other arithmetic  39.5 us (6%)
  local copies, waits for them, and re-layouts  17.8 us (3%)
  matrix products  17.1 us (3%)
  between operations  15.4 us (3%)
  starting transfers between devices  12.8 us (2%)
    all_gather x1, waiting for transfers between devices, per_device(): weights = lax.all_gather(in_weight, 'dp', axis=0, tiled=True)  168 us
    psum x1, waiting for transfers between devices, per_device(): kernel_grad = lax.psum(kernel_part, ('dp', 'seq'))  105 us
    psum x1, waiting for transfers between devices, per_device(): weight_grad = lax.psum(local_rows, 'seq')  91.3 us
    psum x1, blocking collectives, per_device(): lax.psum(jnp.sum(centered * centered, axis=0), ('dp', 'seq')) / counted  42.5 us
    psum x1, blocking collectives, per_device(): lax.psum(jnp.sum(conv_out * valid_mask, axis=0), ('dp', 'seq')) / counted  40.2 us
    psum x1, blocking collectives, per_device(): lax.psum((jnp.sum(grad_shaped, axis=0), jnp.sum(grad_shaped * normed, axi...  38.3 us
    all_to_all x1, waiting for transfers between devices, per_device(): lax.all_to_all(grad_pre[None], 'dp', split_axis=2, concat_axis=0, tiled=T...  18.3 us
    unnamed x1, other arithmetic  17 us
  transfers between devices with their start and end apart: 9, of which 4 were waited for; matrix products, arithmetic and copies ran while one was open for 8% of the time, Pallas kernels for 0%

commit v1 on v0

--- a/solution.py
+++ b/solution.py
@@ -51,7 +51,9 @@
         :, None
     ]
     restored = restore(saved_codes[0], code_scales[0])
-    weights = lax.all_gather(in_weight, "dp", axis=0, tiled=True)
+    weights = jnp.concatenate(
+        lax.all_to_all(jnp.stack([in_weight] * lax.axis_size("dp")), "dp", 0, 0), axis=0
+    )
     pre_act = lax.dot_general(
         restored, weights, (((1,), (1,)), ((), ())), preferred_element_type=jnp.float32
     )

time: 609 us -> 651 us (1.069)
  waiting for transfers between devices: 384 us -> 413 us
    all_to_all x0 -> x1, waiting for transfers between devices: none -> 204 us  [per_device(): lax.all_to_all(jnp.stack([in_weight] * lax.axis_size('dp')), 'dp', 0, 0)]
    all_gather x1 -> x0, waiting for transfers between devices: 168 us -> none  [per_device(): weights = lax.all_gather(in_weight, 'dp', axis=0, tiled=True)]
  transfers between devices with their start and end apart: 9 -> 9, of which waited for: 4 -> 4; matrix products, arithmetic and copies ran while one was open for 8% -> 7% of each run, Pallas kernels for 0% -> 0%
where the time goes in v1:
time: 651 us; the launch traced here: 650 us
  waiting for transfers between devices  413 us (63%)
  blocking collectives  120 us (18%)
  other arithmetic  39.5 us (6%)
  local copies, waits for them, and re-layouts  23.7 us (4%)
  starting transfers between devices  19.3 us (3%)
  matrix products  17.1 us (3%)
  between operations  17.1 us (3%)
    all_to_all x1, waiting for transfers between devices, per_device(): lax.all_to_all(jnp.stack([in_weight] * lax.axis_size('dp')), 'dp', 0, 0)  204 us
    psum x1, waiting for transfers between devices, per_device(): kernel_grad = lax.psum(kernel_part, ('dp', 'seq'))  99.9 us
    psum x1, waiting for transfers between devices, per_device(): weight_grad = lax.psum(local_rows, 'seq')  91 us
    psum x1, blocking collectives, per_device(): lax.psum(jnp.sum(centered * centered, axis=0), ('dp', 'seq')) / counted  42.3 us
    psum x1, blocking collectives, per_device(): lax.psum(jnp.sum(conv_out * valid_mask, axis=0), ('dp', 'seq')) / counted  39.4 us
    psum x1, blocking collectives, per_device(): lax.psum((jnp.sum(grad_shaped, axis=0), jnp.sum(grad_shaped * normed, axi...  38.6 us
    all_to_all x1, waiting for transfers between devices, per_device(): lax.all_to_all(grad_pre[None], 'dp', split_axis=2, concat_axis=0, tiled=T...  18.3 us
    unnamed x1, other arithmetic  17 us
  transfers between devices with their start and end apart: 9, of which 4 were waited for; matrix products, arithmetic and copies ran while one was open for 7% of the time, Pallas kernels for 0%

profile of v1, /device:TPU:0, one launch (start us, length us, event | category | flops | bytes accessed | tf_op | source)
XLA Modules:
  0.0 650.2 jit_solution(4459896051274196234)
XLA Ops:
  8.0 6.1 stack.103
  14.1 6.5 all-to-all-start
  23.2 204.1 %all-to-all-done = bf16[4,768,1536]{2,1,0:T(8,128)(2,1)} async-done(((bf16[4,768,1536]{2,1,0:T(8,128)(2,1)}), bf16[4,768,1536]{2,1,0:T(8,128)(2,1)}, u32[]{:S(2)}, u32[]{:S(2)}) %all-to-all-start) | async-done | bytes 9437216 | tf_op jit(solution)/shard_map/all_to_all | solution.py:55
  227.3 6.9 %fusion.197 = f32[128,3072]{1,0:T(8,128)S(1)} fusion(bf16[128,1536]{0,1:T(8,128)(2,1)S(1)} %bitcast.45, bf16[3072,1536]{1,0:T(8,128)(2,1)} %bitcast.3), kind=kOutput, calls=%fused_computation.396 | convolution fusion | flops 1207959552 | bytes 11403264 | tf_op jit(solution)/shard_map/dot_general | solution.py:57
  234.5 1.4 collective-permute-start.1
  235.9 3.0 collective-permute-start
  240.6 5.1 multiply_reduce_fusion.2
  245.6 39.4 %psum.42 = f32[1536]{0:T(1024)S(1)} all-reduce(f32[1536]{0:T(1024)S(1)} %get-tuple-element.78), channel_id=1, replica_groups=mesh['dp'=4,'seq'=8] {'dp','seq'}, use_global_device_ids=true, to_apply=%region_2.3 | all-reduce | flops 1536 | bytes 12288 | tf_op jit(solution)/shard_map/psum | solution.py:65
  285.2 42.3 %psum.43 = f32[1536]{0:T(1024)S(1)} all-reduce(f32[1536]{0:T(1024)S(1)} %multiply_reduce_fusion.1), channel_id=1, replica_groups=mesh['dp'=4,'seq'=8] {'dp','seq'}, use_global_device_ids=true, to_apply=%region_5.6 | all-reduce | flops 1536 | bytes 12288 | tf_op jit(solution)/shard_map/psum | solution.py:67
  327.5 1.3 fusion.193
  330.1 38.6 %all-reduce = (f32[1536]{0:T(1024)}, f32[1536]{0:T(1024)}) all-reduce(f32[1536]{0:T(1024)S(1)} %get-tuple-element.36, f32[1536]{0:T(1024)S(1)} %get-tuple-element.35), channel_id=1, replica_groups=mesh['dp'=4,'seq'=8] {'dp','seq'}, use_global_device_ids=true, to_apply=%region_9.10 | all-reduce | flops 3072 | bytes 24576 | tf_op jit(solution)/shard_map/psum | solution.py:75
  368.7 3.8 fusion.148
  373.8 3.2 collective-permute-start.2
  379.1 5.3 multiply_convert_fusion.1
  385.6 1.9 copy.22
  388.0 17.0 %reduce.62 = bf16[3072,128]{1,0:T(8,128)(2,1)S(1)} reduce(bf16[3072,1,128]{2,1,0:T(2,128)(2,1)S(1)} %bitcast.41, bf16[]{:T(256)} %broadcast.73), dimensions={1}, to_apply=%bitcast.32.reduce_sub_computation | reduce | bytes 1572866
  406.0 3.5 all-to-all-start.1
  412.8 2.8 stack.135
  415.9 18.3 %all-to-all-done.1 = bf16[4,2,49152]{2,1,0:T(2,128)(2,1)S(1)} async-done(((bf16[4,2,49152]{2,1,0:T(2,128)(2,1)}), bf16[4,2,49152]{2,1,0:T(2,128)(2,1)S(1)}, u32[]{:S(2)}, u32[]{:S(2)}) %all-to-all-start.1) | async-done | bytes 786464 | tf_op jit(solution)/shard_map/all_to_all | solution.py:94
  435.0 4.4 convolution_bitcast_fusion
  440.6 5.9 fusion
  446.4 99.9 %all-reduce.6.cloned.1.call-done = f32[31,1536]{1,0:T(8,128)} async-done(((f32[31,1536]{1,0:T(8,128)}), f32[31,1536]{1,0:T(8,128)}) %all-reduce.6.cloned.1.call-update) | async-done | bytes 190480 | tf_op jit(solution)/shard_map/psum | solution.py:87
  546.3 91.0 %all-reduce.4.cloned.1.call-done = f32[768,1536]{1,0:T(8,128)} async-done(((f32[768,1536]{1,0:T(8,128)}), f32[768,1536]{1,0:T(8,128)}) %all-reduce.4.cloned.1.call-update) | async-done | bytes 4718608 | tf_op jit(solution)/shard_map/psum | solution.py:101
  637.3 4.8 copy.30
  (150 shorter events, 16.8 us)
Async XLA Ops:
  14.1 213.3 %all-to-all-start = ((bf16[4,768,1536]{2,1,0:T(8,128)(2,1)}), bf16[4,768,1536]{2,1,0:T(8,128)(2,1)}, u32[]{:S(2)}, u32[]{:S(2)}) async-start(bf16[4,768,1536]{2,1,0:T(8,128)(2,1)} %stack.103), calls=%async_computation | async-start | bytes 18874368 | tf_op jit(solution)/shard_map/all_to_all | solution.py:55
  20.6 414.5 %all-gather.2.cloned.1.call-start = ((), (), s32[]{:S(2)}) async-start(), calls=%async_computation.2 | async-start | bytes 1966080 | tf_op jit(solution)/shard_map/all_gather | solution.py:97
  20.8 206.5 %copy-start = (bf16[1,128,1536]{1,2,0:T(8,128)(2,1)}, bf16[1,128,1536]{1,2,0:T(8,128)(2,1)S(1)}, u32[]{:S(2)}) copy-start(bf16[1,128,1536]{1,2,0:T(8,128)(2,1)S(1)} %copy.21) | copy-start | bytes 1179652
  22.1 212.1 %copy-start.37 = (f32[128]{0:T(128)}, f32[128]{0:T(128)S(1)}, u32[]{:S(2)}) copy-start(f32[128]{0:T(128)S(1)} %compare_convert_fusion) | copy-start | bytes 1540
  23.0 217.4 %copy-start.13 = (f32[1536]{0:T(1024)}, f32[1536]{0:T(1024)S(1)}, u32[]{:S(2)}) copy-start(f32[1536]{0:T(1024)S(1)} %get-tuple-element.38) | copy-start | bytes 18436
  23.0 217.4 %copy-start.15 = (f32[1536]{0:T(1024)}, f32[1536]{0:T(1024)S(1)}, u32[]{:S(2)}) copy-start(f32[1536]{0:T(1024)S(1)} %get-tuple-element.39) | copy-start | bytes 18436
  23.1 217.4 %copy-start.16 = (f32[1536]{0:T(1024)}, f32[1536]{0:T(1024)S(1)}, u32[]{:S(2)}) copy-start(f32[1536]{0:T(1024)S(1)} %get-tuple-element.40) | copy-start | bytes 18436
  23.1 217.4 %copy-start.17 = (f32[1536]{0:T(1024)}, f32[1536]{0:T(1024)S(1)}, u32[]{:S(2)}) copy-start(f32[1536]{0:T(1024)S(1)} %get-tuple-element.41) | copy-start | bytes 18436
  23.1 217.4 %copy-start.18 = (f32[1536]{0:T(1024)}, f32[1536]{0:T(1024)S(1)}, u32[]{:S(2)}) copy-start(f32[1536]{0:T(1024)S(1)} %get-tuple-element.42) | copy-start | bytes 18436
  23.1 217.4 %copy-start.19 = (f32[1536]{0:T(1024)}, f32[1536]{0:T(1024)S(1)}, u32[]{:S(2)}) copy-start(f32[1536]{0:T(1024)S(1)} %get-tuple-element.43) | copy-start | bytes 18436
  23.1 217.4 %copy-start.20 = (f32[1536]{0:T(1024)}, f32[1536]{0:T(1024)S(1)}, u32[]{:S(2)}) copy-start(f32[1536]{0:T(1024)S(1)} %get-tuple-element.44) | copy-start | bytes 18436
  23.1 217.4 %copy-start.21 = (f32[1536]{0:T(1024)}, f32[1536]{0:T(1024)S(1)}, u32[]{:S(2)}) copy-start(f32[1536]{0:T(1024)S(1)} %get-tuple-element.45) | copy-start | bytes 18436
  23.1 217.4 %copy-start.22 = (f32[1536]{0:T(1024)}, f32[1536]{0:T(1024)S(1)}, u32[]{:S(2)}) copy-start(f32[1536]{0:T(1024)S(1)} %get-tuple-element.46) | copy-start | bytes 18436
  23.1 217.4 %copy-start.23 = (f32[1536]{0:T(1024)}, f32[1536]{0:T(1024)S(1)}, u32[]{:S(2)}) copy-start(f32[1536]{0:T(1024)S(1)} %get-tuple-element.47) | copy-start | bytes 18436
  23.1 217.4 %copy-start.24 = (f32[1536]{0:T(1024)}, f32[1536]{0:T(1024)S(1)}, u32[]{:S(2)}) copy-start(f32[1536]{0:T(1024)S(1)} %get-tuple-element.48) | copy-start | bytes 18436
  23.1 217.4 %copy-start.25 = (f32[1536]{0:T(1024)}, f32[1536]{0:T(1024)S(1)}, u32[]{:S(2)}) copy-start(f32[1536]{0:T(1024)S(1)} %get-tuple-element.49) | copy-start | bytes 18436
  23.1 217.4 %copy-start.26 = (f32[1536]{0:T(1024)}, f32[1536]{0:T(1024)S(1)}, u32[]{:S(2)}) copy-start(f32[1536]{0:T(1024)S(1)} %get-tuple-element.50) | copy-start | bytes 18436
  234.5 5.9 collective-permute-start.1
  235.9 4.5 collective-permute-start
  372.5 6.6 %collective-permute-start.3 = (f32[15,1536]{1,0:T(8,128)S(1)}, f32[15,1536]{1,0:T(8,128)S(1)}, u32[]{:S(2)}, u32[]{:S(2)}) collective-permute-start(f32[15,1536]{1,0:T(8,128)S(1)} %get-tuple-element.81), channel_id=1, source_target_pairs={{1,0},{2,1},{3,2},{4,3},{5,4},{6,5},{7,6},{9,8},{10,9},{11,10},{12... | collective-permute-start | bytes 276488 | tf_op jit(solution)/shard_map/ppermute | solution.py:19
  373.8 5.3 collective-permute-start.2
  406.0 28.2 %all-to-all-start.1 = ((bf16[4,2,49152]{2,1,0:T(2,128)(2,1)}), bf16[4,2,49152]{2,1,0:T(2,128)(2,1)S(1)}, u32[]{:S(2)}, u32[]{:S(2)}) async-start(bf16[4,2,49152]{2,1,0:T(2,128)(2,1)} %reshape.117), calls=%async_computation.1 | async-start | bytes 1572864 | tf_op jit(solution)/shard_map/all_to_all | solution.py:94
  409.5 136.8 %all-reduce.6.cloned.1.call-start = ((), (), s32[]{:S(2)}) async-start(), calls=%async_computation.4 | async-start | bytes 393216 | tf_op jit(solution)/shard_map/psum | solution.py:87
  415.6 221.7 %all-reduce.4.cloned.1.call-start = ((), (), s32[]{:S(2)}) async-start(), calls=%async_computation.3 | async-start | bytes 9437184 | tf_op jit(solution)/shard_map/psum | solution.py:101
  (26 other events, 521.0 us)
Sparse Core Ops, SparseCore 0:
  379.2 43.8 all-gather.1
Sparse Core Ops, SparseCore 1:
  416.1 130.2 all-reduce.5
  550.1 87.1 all-reduce.3
